TPU v7x, 256 devices: a whole 4x4x8 slice. The times are simulated.
256 devices in a mesh: row: 32 (over z, x), col: 8 (over y, core).
Axes of the slice: x: 4, y: 4, z: 8, core: 2. Of those that a mesh axis runs over, the one named last changes fastest.
Arguments:
- schur: float32 [2, 32768, 4096], P(None, 'row', 'col'), may hold values from -6 to 6
- lower: bfloat16 [2, 32768, 2048], P(None, 'row', 'col'), may hold values from -6 to 6
- upper: bfloat16 [2, 2048, 4096], P(None, 'row', 'col'), may hold values from -0.1875 to 0.1875
- tile_mask: int32 [2, 256, 16], P(None, 'row', 'col'), may hold values from 0 to 1, as said below
- row_map: int32 [2, 32768], P(None, 'row'), may hold values from 0 to 32767, as said below
- front: float32 [32768, 4096], P('row', 'col'), may hold values from -6 to 6
Outputs:
- front_out: float32 [32768, 4096], P('row', 'col')
Inputs may be any that keep to these rules, and one draw needn't show every extreme that they name: `tile_mask`: in every row of tiles of each child, each aligned pair of tile columns (2 j, 2 j + 1) holds exactly one 1. `row_map`: for each child a permutation of the 32768 rows. Of the 1024 rows of any aligned block, at least 16 and at most 48 map into any one aligned block of 1024 parent rows; some pair of blocks reaches 48.
All inputs are finite; a program needn't handle non-finite values.
Results may differ from a plain program's by a relative error of at most 0.0003.
Values may be sent and summed in bfloat16 or wider, within the bound.
A program may use at most 128 MiB of HBM per device.

v0:
```python
import jax
import jax.numpy as jnp
from jax import lax
from jax.sharding import Mesh
from jax.sharding import PartitionSpec as P

TILE = 128
ROW = ("row_0", "row_1")


def gathered_by_axis(array, axes, dim):
    result = array
    for number in range(len(axes) - 1, -1, -1):
        result = lax.all_gather(result, axes[number], axis=dim, tiled=True)
    return result


def build_send(contrib, maps, count):
    children, rows, width = contrib.shape
    cap = 3 * rows // (2 * count)
    target = maps // rows
    place = maps % rows
    onehot = (target[:, :, None] == jnp.arange(count, dtype=jnp.int32)[None, None, :]).astype(
        jnp.int32
    )
    ranks = jnp.cumsum(onehot, axis=1) - 1
    slot = jnp.sum(ranks * onehot, axis=2)
    flat = target * cap + slot
    child_ids = jnp.arange(children, dtype=jnp.int32)[:, None]
    values = jnp.zeros((children, count * cap, width), jnp.float32).at[child_ids, flat].set(contrib)
    places = (
        jnp.full((children, count * cap), float(rows), jnp.float32)
        .at[child_ids, flat]
        .set(place.astype(jnp.float32))
    )
    return (values.reshape(children, count, cap, width), places.reshape(children, count, cap))


def assemble(result, values, places):
    width = values.shape[-1]
    index = places.reshape(-1).astype(jnp.int32)
    return result.at[index].add(values.reshape(-1, width), mode="drop")


def shards(schur, lower, upper, tile_mask, row_map, front):
    children, rows, local_depth = lower.shape
    width = schur.shape[2]
    row_tiles = rows // TILE
    local_tiles = local_depth // TILE
    upper_full = gathered_by_axis(upper, ROW, 1)
    local_pairs = local_tiles // 2
    lower_six = lower.reshape(children, row_tiles, TILE, local_pairs, 2, TILE)
    weight_six = tile_mask.reshape(children, row_tiles, 1, local_pairs, 2, 1).astype(jnp.bfloat16)
    packed = jnp.sum(lower_six * weight_six, axis=4).reshape(children, rows, local_pairs * TILE)
    flags = tile_mask.reshape(children, row_tiles, local_pairs, 2)[..., 1].astype(jnp.bfloat16)
    packed_full, flags_full = (
        lax.all_gather(packed, "col", axis=2, tiled=True),
        lax.all_gather(flags, "col", axis=2, tiled=True),
    )
    total_pairs = flags_full.shape[2]
    upper_pairs = upper_full.reshape(children, total_pairs, 2, TILE, width)
    packed_five = packed_full.reshape(children, row_tiles, TILE, total_pairs, TILE)
    update = jnp.zeros((children, rows, width), jnp.float32)
    for parity in range(2):
        select = (flags_full == float(parity)).astype(jnp.bfloat16)
        chosen = (packed_five * select[:, :, None, :, None]).reshape(
            children, rows, total_pairs * TILE
        )
        panel = upper_pairs[:, :, parity].reshape(children, total_pairs * TILE, width)
        update = update + jnp.einsum(
            "cmk,ckw->cmw", chosen, panel, preferred_element_type=jnp.float32
        )
    contrib = schur - update
    count = lax.axis_size(ROW)
    result = front
    values, places = build_send(contrib, row_map, count)
    got_values, got_places = (
        lax.all_to_all(values, ROW, split_axis=1, concat_axis=1, tiled=True),
        lax.all_to_all(places, ROW, split_axis=1, concat_axis=1, tiled=True),
    )
    result = assemble(result, got_values, got_places)
    return result


def solution(mesh):
    split = Mesh(mesh.devices.reshape(8, 4, mesh.shape["col"]), ("row_0", "row_1", "col"))
    in_specs = (
        P(None, ROW, "col"),
        P(None, ROW, "col"),
        P(None, ROW, "col"),
        P(None, ROW, "col"),
        P(None, ROW),
        P(ROW, "col"),
    )
    out_specs = P(ROW, "col")
    return jax.shard_map(
        shards, mesh=split, in_specs=in_specs, out_specs=out_specs, check_vma=False
    )
```

profile of v0, /device:TPU:16, one launch (start us, length us, event | category | flops | bytes accessed | tf_op | source)
XLA Modules:
  0.0 339.2 jit_solution(4166249342058747314)
XLA Ops:
  6.5 0.0 copy-start.4
  6.5 0.0 copy-start.3
  6.5 0.0 copy-start.6
  6.5 0.0 copy-start.5
  6.5 0.0 all-gather.6.cloned.1.call-start
  6.6 3.2 copy.65
  9.8 0.0 copy-done.4
  9.8 0.0 copy-start.7
  9.8 0.0 copy-start.8
  9.8 14.0 %all_gather.14 = bf16[2,256,512]{2,1,0:T(8,128)(2,1)} all-gather(bf16[2,64,512]{2,1,0:T(8,128)(2,1)S(1)} %copy-done.4), channel_id=1, replica_groups=mesh['row_0'=8,'row_1'=4,'col'=8] {'row_1'}, dimensions={1}, use_global_device_ids=true | all-gather | bytes 655360 | tf_op jit(solution)/shard_map/all_gather | solution.py:14
  23.8 0.0 all-gather.6.cloned.1.call-update
  23.8 0.0 all-gather.4.cloned.1.call-start
  23.8 0.0 copy-done.3
  23.8 0.3 reshape.99
  24.1 0.0 copy-done.6
  24.2 0.1 copy.43
  24.3 3.7 %multiply_reduce_fusion = bf16[2,8,128,128]{3,2,1,0:T(8,128)(2,1)} fusion(bf16[2,8,128,1,2,128]{5,4,2,1,0,3:T(2,128)(2,1)S(1)} %reshape.99, bf16[2,8,2]{2,1,0:T(8,128)(2,1)S(1)} %copy.43), kind=kLoop, calls=%fused_computation.10 | loop fusion | flops 786432 | bytes 1572928 | tf_op jit(solution)/shard_map/reduce_sum | solution.py:54
  28.0 0.0 all-gather.4.cloned.1.call-update
  28.0 0.0 copy-done.5
  28.1 18.0 %reduce-window.6 = s32[2,32,8,128]{3,2,1,0:T(8,128)S(1)} reduce-window(s32[2,32,8,128]{3,2,1,0:T(8,128)S(1)} %fusion.9, s32[]{:T(128)} %constant.45.clone.1), window={size=1x1x1x128 pad=0_0x0_0x0_0x127_0}, to_apply=%region_0.0 | reduce-window | flops 8323072 | bytes 524292 | tf_op jit(solution)/shard_map/reduce-window
  46.1 0.1 slice.21
  46.3 0.2 copy.39
  46.5 0.1 copy.40
  46.6 0.1 add_add_fusion
  46.8 0.1 fusion.8
  46.9 0.0 copy-done.7
  46.9 0.1 multiply_reduce_fusion.1
  47.0 0.0 copy-done.8
  47.0 0.1 and_reduce_fusion
  47.1 8.1 %scatter_custom_fusion.1 = f32[3072]{0:T(1024)S(1)} fusion(s32[2048]{0:T(1024)S(1)} %bitcast.58, f32[2048]{0:T(1024)S(1)} %bitcast.60, f32[]{:T(128)} %constant.43.clone.1), kind=kCustom, calls=%fused_computation.37 | custom fusion | bytes 12292
  55.2 0.1 reshape.98
  55.2 0.6 copy.41
  55.9 11.4 %all-to-all-start = ((f32[2,32,48]{2,0,1:T(2,128)}), f32[2,32,48]{2,0,1:T(2,128)S(1)}, u32[]{:S(2)}, u32[]{:S(2)}) async-start(f32[2,32,48]{2,0,1:T(2,128)} %copy.41), calls=%async_computation | async-start | bytes 65536 | tf_op jit(solution)/shard_map/all_to_all | solution.py:79
  67.3 8.7 %all-gather = bf16[2,8,8,1]{1,0,3,2:T(2,128)(2,1)S(1)} all-gather(bf16[2,8,1,1]{1,0,3,2:T(2,128)(2,1)S(1)} %copy.44), channel_id=2, replica_groups=mesh['row_0'=8,'row_1'=4,'col'=8] {'col'}, dimensions={2}, use_global_device_ids=true | all-gather | bytes 288 | tf_op jit(solution)/shard_map/all_gather | solution.py:58
  75.9 0.1 copy.45
  76.0 2.6 mul.55
  78.6 7.3 %mul.56 = bf16[2,1024,1024]{2,1,0:T(8,128)(2,1)} reshape(bf16[2,8,128,8,128]{4,3,2,1,0:T(8,128)(2,1)} %mul.55) | data formatting | bytes 8388608 | tf_op jit(solution)/shard_map/mul | solution.py:66
  85.9 2.5 mul.52
  88.5 7.3 %mul.53 = bf16[2,1024,1024]{2,1,0:T(8,128)(2,1)} reshape(bf16[2,8,128,8,128]{4,3,2,1,0:T(8,128)(2,1)} %mul.52) | data formatting | bytes 8388608 | tf_op jit(solution)/shard_map/mul | solution.py:66
  95.8 0.0 all-gather.6.cloned.1.call-done
  95.8 4.1 %fusion.17 = (bf16[2,8,1,128,512]{4,3,2,1,0:T(8,128)(2,1)S(1)}, bf16[2,8,1,128,512]{4,3,2,1,0:T(8,128)(2,1)}) fusion(bf16[2,8,2,128,512]{4,3,2,1,0:T(8,128)(2,1)} %bitcast.50), kind=kLoop, calls=%fused_computation.43 | loop fusion | bytes 8388608 | tf_op jit(solution)/shard_map/slice | solution.py:69
  99.8 20.6 %all-gather.4.cloned.1.call-done = bf16[2,1024,1024]{2,1,0:T(8,128)(2,1)} async-done(((bf16[2,1024,128]{2,1,0:T(8,128)(2,1)}), bf16[2,1024,1024]{2,1,0:T(8,128)(2,1)}) %all-gather.4.cloned.1.call-update) | async-done | bytes 4194320 | tf_op jit(solution)/shard_map/all_gather | solution.py:57
  120.5 0.0 copy-start
  120.5 0.0 copy-start.1
  120.5 0.0 copy-start.2
  120.5 6.5 %fusion = f32[2,1024,512]{2,1,0:T(8,128)S(1)} fusion(bf16[2,1024,512]{2,1,0:T(8,128)(2,1)} %bitcast.53, bf16[2,1024,1024]{2,1,0:T(8,128)(2,1)} %all-gather.4.cloned.1.call-done, bf16[2,1024,1024]{2,1,0:T(8,128)(2,1)} %mul.56), kind=kOutput, calls=%fused_computation.4 | convolution fusion | flops 2149580800 | bytes 14680064 | tf_op jit(solution)/shard_map/cmk,ckw->cmw/dot_general | solution.py:70
  127.0 0.0 copy-done
  127.0 0.0 copy-done.1
  127.0 1.2 copy-done.2
  128.2 4.3 %add_subtract_fusion = f32[2,1024,512]{2,1,0:T(8,128)} fusion(f32[2,1024,512]{2,1,0:T(8,128)S(1)} %copy-done.1, f32[2,1024,512]{2,1,0:T(8,128)S(1)} %fusion, bf16[2,1024,512]{2,1,0:T(8,128)(2,1)S(1)} %bitcast.49, bf16[2,1024,1024]{2,1,0:T(8,128)(2,1)S(1)} %copy-done.2, bf16[2,1024,1024]{2,1,0:T(8,128)(2,1)S(1)} %copy-done), kind=kOutput, calls=%fused_computation.3 | convolution fusion | flops 2151677952 | bytes 23068672 | tf_op jit(solution)/shard_map/cmk,ckw->cmw/dot_general | solution.py:70
  132.4 12.7 %scatter_custom_fusion.2 = f32[3072,512]{1,0:T(8,128)} fusion(s32[2048]{0:T(1024)S(1)} %bitcast.59, f32[2048,512]{1,0:T(8,128)} %bitcast.51, f32[]{:T(128)} %constant.52.clone.1), kind=kCustom, calls=%fused_computation.8 | custom fusion | bytes 6291968
  145.1 6.7 %copy.49 = f32[2,32,48,512]{3,2,0,1:T(8,128)} copy(f32[2,32,48,512]{3,2,1,0:T(8,128)} %bitcast.47) | data formatting | bytes 12582912 | tf_op jit(solution)/shard_map/reshape | solution.py:36
  151.8 0.0 all-to-all-done
  151.8 10.2 %all-to-all-start.1 = ((f32[2,32,48,512]{3,2,0,1:T(8,128)}), f32[2,32,48,512]{3,2,0,1:T(8,128)}, u32[]{:S(2)}, u32[]{:S(2)}) async-start(f32[2,32,48,512]{3,2,0,1:T(8,128)} %copy.49), calls=%async_computation.1 | async-start | bytes 12582912 | tf_op jit(solution)/shard_map/all_to_all | solution.py:78
  162.0 0.1 convert_element_type.48
  162.1 141.4 %all-to-all-done.1 = f32[2,32,48,512]{3,2,0,1:T(8,128)} async-done(((f32[2,32,48,512]{3,2,0,1:T(8,128)}), f32[2,32,48,512]{3,2,0,1:T(8,128)}, u32[]{:S(2)}, u32[]{:S(2)}) %all-to-all-start.1) | async-done | bytes 6291488 | tf_op jit(solution)/shard_map/all_to_all | solution.py:78
  303.5 6.8 %copy.50 = f32[2,32,48,512]{3,2,1,0:T(8,128)} copy(f32[2,32,48,512]{3,2,0,1:T(8,128)} %all-to-all-done.1) | data formatting | bytes 12582912 | tf_op jit(solution)/shard_map/all_to_all | solution.py:78
  310.3 22.1 %scatter_fusion = f32[1024,512]{1,0:T(8,128)} fusion(f32[1024,512]{1,0:T(8,128)} %copy.65, s32[3072]{0:T(1024)S(1)} %bitcast.55, f32[3072,512]{1,0:T(8,128)} %bitcast.48), kind=kCustom, calls=%fused_computation | custom fusion | flops 1572864 | bytes 18886656 | tf_op jit(solution)/shard_map/scatter-add | solution.py:42
  (18 shorter events, 0.2 us)
Async XLA Ops:
  6.5 3.2 copy-start.4
  6.5 17.3 %copy-start.3 = (bf16[2,1024,256]{2,1,0:T(8,128)(2,1)S(1)}, bf16[2,1024,256]{2,1,0:T(8,128)(2,1)}, u32[]{:S(2)}) copy-start(bf16[2,1024,256]{2,1,0:T(8,128)(2,1)} %param.7) | copy-start | bytes 3145732
  6.5 17.6 %copy-start.6 = (s32[2,8,2]{1,2,0:T(2,128)S(1)}, s32[2,8,2]{1,2,0:T(2,128)}, u32[]{:S(2)}) copy-start(s32[2,8,2]{1,2,0:T(2,128)} %param.9) | copy-start | bytes 388
  6.5 21.5 %copy-start.5 = (s32[2,1024]{1,0:T(2,128)S(1)}, s32[2,1024]{1,0:T(2,128)}, u32[]{:S(2)}) copy-start(s32[2,1024]{1,0:T(2,128)} %param.10) | copy-start | bytes 24580
  6.5 89.2 %all-gather.6.cloned.1.call-start = ((), (), s32[]{:S(2)}) async-start(), calls=%async_computation.3 | async-start | bytes 4718592 | tf_op jit(solution)/shard_map/all_gather | solution.py:14
  9.8 37.1 %copy-start.7 = (s32[2]{0:T(128)S(1)}, s32[2]{0:T(128)}, u32[]{:S(2)}) copy-start(s32[2]{0:T(128)} %constant.56) | copy-start | bytes 28
  9.8 37.2 %copy-start.8 = (s32[2]{0:T(128)S(1)}, s32[2]{0:T(128)}, u32[]{:S(2)}) copy-start(s32[2]{0:T(128)} %constant.59) | copy-start | bytes 28
  23.8 96.7 %all-gather.4.cloned.1.call-start = ((), (), s32[]{:S(2)}) async-start(), calls=%async_computation.2 | async-start | bytes 4718592 | tf_op jit(solution)/shard_map/all_gather | solution.py:57
  55.9 96.0 %all-to-all-start = ((f32[2,32,48]{2,0,1:T(2,128)}), f32[2,32,48]{2,0,1:T(2,128)S(1)}, u32[]{:S(2)}, u32[]{:S(2)}) async-start(f32[2,32,48]{2,0,1:T(2,128)} %copy.41), calls=%async_computation | async-start | bytes 65536 | tf_op jit(solution)/shard_map/all_to_all | solution.py:79
  120.5 6.5 %copy-start = (bf16[2,1024,1024]{2,1,0:T(8,128)(2,1)S(1)}, bf16[2,1024,1024]{2,1,0:T(8,128)(2,1)}, u32[]{:S(2)}) copy-start(bf16[2,1024,1024]{2,1,0:T(8,128)(2,1)} %mul.53) | copy-start | bytes 12582916
  120.5 6.5 %copy-start.1 = (f32[2,1024,512]{2,1,0:T(8,128)S(1)}, f32[2,1024,512]{2,1,0:T(8,128)}, u32[]{:S(2)}) copy-start(f32[2,1024,512]{2,1,0:T(8,128)} %param.6) | copy-start | bytes 12582916
  120.5 7.7 %copy-start.2 = (bf16[2,1024,1024]{2,1,0:T(8,128)(2,1)S(1)}, bf16[2,1024,1024]{2,1,0:T(8,128)(2,1)}, u32[]{:S(2)}) copy-start(bf16[2,1024,1024]{2,1,0:T(8,128)(2,1)} %all-gather.4.cloned.1.call-done) | copy-start | bytes 12582916
  151.8 151.7 %all-to-all-start.1 = ((f32[2,32,48,512]{3,2,0,1:T(8,128)}), f32[2,32,48,512]{3,2,0,1:T(8,128)}, u32[]{:S(2)}, u32[]{:S(2)}) async-start(f32[2,32,48,512]{3,2,0,1:T(8,128)} %copy.49), calls=%async_computation.1 | async-start | bytes 12582912 | tf_op jit(solution)/shard_map/all_to_all | solution.py:78
Sparse Core Ops, SparseCore 0:
  23.9 58.3 all-gather.5
  84.1 36.3 all-gather.3
where the time goes:
time: 344 us; the launch traced here: 339 us
  waiting for transfers between devices  162 us (47%)
  local copies, waits for them, and re-layouts  64.1 us (19%)
  other arithmetic  44.3 us (13%)
  blocking collectives  22.6 us (7%)
  starting transfers between devices  21.6 us (6%)
  between operations  13.7 us (4%)
  matrix products  10.8 us (3%)
    all_to_all x1, waiting for transfers between devices, shards(): lax.all_to_all(values, ROW, split_axis=1, concat_axis=1, tiled=True)  141 us
    unnamed x24, local copies, waits for them, and re-layouts  25.1 us
    scatter-add x1, other arithmetic, assemble(): return result.at[index].add(values.reshape(-1, width), mode='drop')  22.1 us
    all_gather x1, waiting for transfers between devices, shards(): lax.all_gather(packed, 'col', axis=2, tiled=True)  20.6 us
    mul x4, local copies, waits for them, and re-layouts, shards(): packed_five * select[:, :, None, :, None]  19.7 us
    another operation x2, other arithmetic  18.1 us
    all_gather x1, blocking collectives, gathered_by_axis(): result = lax.all_gather(result, axes[number], axis=dim, tiled=True)  14 us
    all_to_all x1, starting transfers between devices, shards(): lax.all_to_all(places, ROW, split_axis=1, concat_axis=1, tiled=True)  11.4 us
  transfers between devices with their start and end apart: 4, of which 2 were waited for; matrix products, arithmetic and copies ran while one was open for 25% of the time, Pallas kernels for 0%

commit v1 on v0

v1 whole, which is shorter than its diff:
```python
import functools

import jax
import jax.numpy as jnp
from jax import lax
from jax.experimental import pallas as pl
from jax.experimental.pallas import tpu as pltpu
from jax.sharding import PartitionSpec as P

TILE = 128
X = 4
CORES = 2
HALVES = 2
MESH = pl.DeviceIdType.MESH
F32 = jnp.float32
BF16 = jnp.bfloat16
I32 = jnp.int32


def dot(a, b):
    return jnp.dot(a, b, preferred_element_type=F32)


def iota(shape, dim):
    return lax.broadcasted_iota(I32, shape, dim)


def kernel(
    dims,
    lower_ref,
    upper_ref,
    mask_ref,
    map_ref,
    schur_hbm,
    front_hbm,
    out_ref,
    schur,
    packed,
    wide,
    panel,
    square,
    hot,
    owner,
    rows_info,
    cols_info,
    place_info,
    scale_col,
    high,
    low,
    code_out,
    code_in,
    meta_out,
    meta_in,
    meta_flat,
    spread,
    high_in,
    low_in,
    local_sem,
    z_send,
    z_recv,
    x_send,
    x_recv,
    y_send,
    y_recv,
    c_send,
    c_recv,
    e_send,
    e_recv,
    m_send,
    m_recv,
):
    count, cols, rows, width, depth, cap = dims
    zs = count // X
    ys = cols // CORES
    cw = width // HALVES
    slots = count * cap
    full = depth * count
    me = lax.axis_index("row")
    col = lax.axis_index("col")
    my_z = me // X
    my_x = lax.rem(me, X)
    my_y = col // CORES
    core = lax.rem(col, CORES)
    partner = my_y * CORES + (1 - core)

    barrier = pltpu.get_barrier_semaphore()

    def greet_row(k, carry):
        pl.semaphore_signal(barrier, inc=1, device_id=(lax.rem(me + k, count), col), device_id_type=MESH)
        return carry

    def greet_col(k, carry):
        pl.semaphore_signal(barrier, inc=1, device_id=(me, lax.rem(col + k, cols)), device_id_type=MESH)
        return carry

    lax.fori_loop(1, count, greet_row, 0)
    lax.fori_loop(1, cols, greet_col, 0)

    schur_copy = pltpu.make_async_copy(schur_hbm, schur, local_sem.at[0])
    front_copy = pltpu.make_async_copy(front_hbm, out_ref, local_sem.at[1])
    schur_copy.start()
    front_copy.start()

    for child in range(2):
        for tile in range(rows // TILE):
            at = pl.ds(tile * TILE, TILE)
            second = mask_ref[child, tile, 1]
            packed[child, col, at, :] = jnp.where(
                second == 1, lower_ref[child, at, TILE : 2 * TILE], lower_ref[child, at, 0:TILE]
            )
        row = iota((16, TILE), 0)
        flags = jnp.zeros((16, TILE), F32)
        for tile in range(rows // TILE):
            flags = jnp.where(row == tile, mask_ref[child, tile, 1].astype(F32), flags)
        packed[child, col, pl.ds(rows, 16), :] = flags.astype(BF16)

    pl.semaphore_wait(barrier, count + cols - 2)

    def upper_block(step):
        child, half = step // HALVES, step % HALVES
        return upper_ref.at[child, :, pl.ds(half * cw, cw)]

    def panel_block(step, z, x):
        start = pl.multiple_of((z * X + x) * depth, depth)
        return panel.at[step, pl.ds(start, depth), :]

    def nearest(n):
        half = n // 2 + 1
        return half + lax.rem(n, 2) * (zs - 2 * half)

    def z_copy(step, dz):
        z = lax.rem(my_z + dz, zs)
        return pltpu.make_async_remote_copy(
            src_ref=upper_block(step),
            dst_ref=panel_block(step, my_z, my_x),
            send_sem=z_send.at[step],
            recv_sem=z_recv.at[step, dz],
            device_id=(z * X + my_x, col),
            device_id_type=MESH,
        )

    def x_copy(step, source, z, dx):
        return pltpu.make_async_remote_copy(
            src_ref=source,
            dst_ref=panel_block(step, z, my_x),
            send_sem=x_send.at[step],
            recv_sem=x_recv.at[step],
            device_id=(my_z * X + lax.rem(my_x + dx, X), col),
            device_id_type=MESH,
        )

    def send_upper(step):
        def body(n, carry):
            z_copy(step, nearest(n)).start()
            return carry

        lax.fori_loop(0, zs - 1, body, 0)
        for dx in (1, 3, 2):
            x_copy(step, upper_block(step), my_z, dx).start()
        pltpu.make_async_copy(upper_block(step), panel_block(step, my_z, my_x), local_sem.at[2 + step]).start()

    def pass_upper(step):
        def body(n, carry):
            dz = nearest(n)
            z_copy(step, dz).wait_recv()
            z = lax.rem(my_z - dz + zs, zs)
            for dx in (1, 3, 2):
                x_copy(step, panel_block(step, z, my_x), z, dx).start()
            return carry

        lax.fori_loop(0, zs - 1, body, 0)

    def wait_upper(step):
        pltpu.make_async_copy(upper_block(step), panel_block(step, my_z, my_x), local_sem.at[2 + step]).wait()
        got = panel.at[step, pl.ds(0, (X - 1) * zs * depth), :]
        pltpu.make_async_remote_copy(
            src_ref=got, dst_ref=got, send_sem=x_send.at[step], recv_sem=x_recv.at[step],
            device_id=(me, partner), device_id_type=MESH,
        ).wait_recv()

    def y_copy(child, dy):
        y = lax.rem(my_y + dy, ys)
        return pltpu.make_async_remote_copy(
            src_ref=packed.at[child, col],
            dst_ref=packed.at[child, col],
            send_sem=y_send.at[child],
            recv_sem=y_recv.at[child, dy],
            device_id=(me, y * CORES + core),
            device_id_type=MESH,
        )

    def c_copy(child, y):
        block = y * CORES + core
        return pltpu.make_async_remote_copy(
            src_ref=packed.at[child, block],
            dst_ref=packed.at[child, block],
            send_sem=c_send.at[child],
            recv_sem=c_recv.at[child],
            device_id=(me, partner),
            device_id_type=MESH,
        )

    def send_lower(child):
        for dy in (1, 3, 2):
            y_copy(child, dy).start()
        c_copy(child, my_y).start()

    def pass_lower(child):
        for dy in (1, 3, 2):
            y_copy(child, dy).wait_recv()
            c_copy(child, lax.rem(my_y - dy + ys, ys)).start()

    def wait_lower(child):
        got = packed.at[child, pl.ds(0, ys)]
        pltpu.make_async_remote_copy(
            src_ref=got, dst_ref=got, send_sem=c_send.at[child], recv_sem=c_recv.at[child],
            device_id=(me, partner), device_id_type=MESH,
        ).wait_recv()

    def index_rows():
        def strict(b, carry):
            at = pl.ds(pl.multiple_of(b * TILE, TILE), TILE)
            before = iota((TILE, rows), 0) + b * TILE < iota((TILE, rows), 1)
            square[at, :] = jnp.where(before, 1.0, 0.0).astype(BF16)
            return carry

        lax.fori_loop(0, rows // TILE, strict, 0)
        for child in range(2):
            line = map_ref[pl.ds(child, 1), :]
            same = iota((count, rows), 0) == line // rows
            owner[child] = jnp.where(same, 1.0, 0.0).astype(BF16)
        rows_info[...] = jnp.zeros_like(rows_info)
        for child in range(2):
            line = map_ref[pl.ds(child, 1), :]
            hits = owner[child]
            ahead = dot(hits, square[...])
            rank = jnp.sum(ahead * hits.astype(F32), axis=0, keepdims=True)
            spot = lax.rem(line, rows) + 1
            rows_info[pl.ds(4 * child, 1), :] = rank
            rows_info[pl.ds(4 * child + 1, 1), :] = (spot // 32).astype(F32)
            rows_info[pl.ds(4 * child + 2, 1), :] = lax.rem(spot, 32).astype(F32)
            rows_info[pl.ds(4 * child + 3, 1), :] = (line // rows).astype(F32)

        def identity(b, carry):
            at = pl.ds(pl.multiple_of(b * TILE, TILE), TILE)
            equal = iota((TILE, rows), 0) + b * TILE == iota((TILE, rows), 1)
            square[at, :] = jnp.where(equal, 1.0, 0.0).astype(BF16)
            return carry

        lax.fori_loop(0, rows // TILE, identity, 0)
        cols_info[...] = lax.dot_general(
            square[...], rows_info[...].astype(BF16), (((1,), (1,)), ((), ())), preferred_element_type=F32
        )
        for child in range(2):
            lane = iota((rows, TILE), 1).astype(F32)
            match = lane - 64.0 == cols_info[:, 4 * child : 4 * child + 1]
            tops = jnp.where(match, cols_info[:, 4 * child + 1 : 4 * child + 2], 0.0).astype(BF16)
            ends = jnp.where(match, cols_info[:, 4 * child + 2 : 4 * child + 3], 0.0).astype(BF16)
            place_info[child] = 32.0 * dot(owner[child], tops) + dot(owner[child], ends)
        slot = iota((TILE, slots), 1).astype(F32)
        inner = slot - cap * jnp.floor((slot + 0.5) * (1.0 / cap))
        lane = iota((TILE, slots), 0).astype(F32)
        spread[0] = jnp.where(lane == inner, 1.0, 0.0).astype(BF16)
        spread[1] = jnp.where(lane - 64.0 == inner, 1.0, 0.0).astype(BF16)

    def build_hot(child):
        flat = rows_info[pl.ds(4 * child + 3, 1), :] * float(cap) + rows_info[pl.ds(4 * child, 1), :]

        def body(b, carry):
            at = pl.ds(pl.multiple_of(b * TILE, TILE), TILE)
            slot = (iota((TILE, rows), 0) + b * TILE).astype(F32)
            hot[at, :] = jnp.where(slot == flat, 1.0, 0.0).astype(BF16)
            return carry

        lax.fori_loop(0, slots // TILE, body, 0)

    def widen(child):
        def body(j, carry):
            flags = packed[child, j, pl.ds(rows, 16), :].astype(F32)
            for tile in range(rows // TILE):
                at = pl.ds(tile * TILE, TILE)
                block = packed[child, j, at, :].astype(F32)
                flag = flags[tile : tile + 1, :]
                left = pl.multiple_of(j * 2 * TILE, TILE)
                right = pl.multiple_of(j * 2 * TILE + TILE, TILE)
                wide[at, pl.ds(left, TILE)] = (block * (1.0 - flag)).astype(BF16)
                wide[at, pl.ds(right, TILE)] = (block * flag).astype(BF16)
            return carry

        lax.fori_loop(0, cols, body, 0)

    def contribute(step):
        child, half = step // HALVES, step % HALVES
        part = rows // 2
        for b in range(2):
            at = pl.ds(b * part, part)
            update = dot(wide[at, :], panel[step])
            value = schur[child, at, pl.ds(half * cw, cw)] - update
            peak = jnp.maximum(jnp.max(jnp.abs(value), axis=1, keepdims=True), 1e-30)
            scale_col[at, :] = jnp.broadcast_to(peak * ((1.0 + 2.0**-8) / 32767.0), (part, TILE)).astype(BF16)
            inverse = 1.0 / scale_col[at, :].astype(F32)
            code = jnp.floor(value * inverse[:, 0:1] + 0.5)
            top = jnp.floor(code * (1.0 / 256.0))
            high[at, :] = top.astype(BF16)
            low[at, :] = (code - 256.0 * top).astype(BF16)
        size = slots // 3
        for b in range(3):
            at = pl.ds(b * size, size)
            code = 256.0 * dot(hot[at, :], high[...]) + dot(hot[at, :], low[...])
            code_out[step, at, :] = code.astype(I32).astype(jnp.int16)
        lane = iota((rows, TILE), 1).astype(F32)
        match = lane == cols_info[:, 4 * child : 4 * child + 1]
        scales = jnp.where(match, scale_col[...].astype(F32), 0.0).astype(BF16)
        meta = dot(owner[child], scales) + place_info[child]
        for t in range(count):
            meta_out[step, t] = meta[t : t + 1, :]

    def rows_of(t):
        return pl.ds(pl.multiple_of(t * cap, 16), cap)

    def e_copy(step, k):
        t = lax.rem(me + k, count)
        return pltpu.make_async_remote_copy(
            src_ref=code_out.at[step, rows_of(t), :],
            dst_ref=code_in.at[step, rows_of(me), :],
            send_sem=e_send.at[step],
            recv_sem=e_recv.at[step],
            device_id=(t, col),
            device_id_type=MESH,
        )

    def m_copy(step, k):
        t = lax.rem(me + k, count)
        return pltpu.make_async_remote_copy(
            src_ref=meta_out.at[step, t],
            dst_ref=meta_in.at[step, me],
            send_sem=m_send.at[step],
            recv_sem=m_recv.at[step],
            device_id=(t, col),
            device_id_type=MESH,
        )

    def own_copies(step):
        return (
            pltpu.make_async_copy(
                code_out.at[step, rows_of(me), :], code_in.at[step, rows_of(me), :], local_sem.at[6 + step]
            ),
            pltpu.make_async_copy(meta_out.at[step, me], meta_in.at[step, me], local_sem.at[10 + step]),
        )

    def exchange(step):
        def body(k, carry):
            e_copy(step, k).start()
            m_copy(step, k).start()
            return carry

        lax.fori_loop(1, count, body, 0)
        for copy in own_copies(step):
            copy.start()

    def all_codes(step):
        got = code_in.at[step, pl.ds(0, (count - 1) * cap), :]
        return pltpu.make_async_remote_copy(
            src_ref=got, dst_ref=got, send_sem=e_send.at[step], recv_sem=e_recv.at[step],
            device_id=(me, partner), device_id_type=MESH,
        )

    def all_meta(step):
        got = meta_in.at[step, pl.ds(0, count - 1)]
        return pltpu.make_async_remote_copy(
            src_ref=got, dst_ref=got, send_sem=m_send.at[step], recv_sem=m_recv.at[step],
            device_id=(me, partner), device_id_type=MESH,
        )

    def collect(step):
        half = step % HALVES
        for copy in own_copies(step):
            copy.wait()
        all_codes(step).wait_recv()
        all_meta(step).wait_recv()
        for s in range(count):
            meta_flat[s : s + 1, :] = meta_in[step, s]
        flat = meta_flat[...]
        tops = jnp.floor(flat * (1.0 / 32.0))
        ends = flat - 32.0 * tops
        places = 32.0 * dot(tops.astype(BF16), spread[1]) + dot(ends.astype(BF16), spread[1])
        scales = dot(flat.astype(BF16), spread[0])
        slot = iota((count, slots), 1)
        first = iota((count, slots), 0) * cap
        own = (slot >= first) & (slot < first + cap)
        place = jnp.sum(jnp.where(own, places, 0.0), axis=0, keepdims=True)
        scale = jnp.sum(jnp.where(own, scales, 0.0), axis=0, keepdims=True)
        size = slots // 3
        for b in range(3):
            at = pl.ds(b * size, size)
            code = code_in[step, at, :].astype(I32)
            high_in[at, :] = (code >> 8).astype(F32).astype(BF16)
            low_in[at, :] = (code & 255).astype(F32).astype(BF16)
        part = rows // 4
        for b in range(4):
            target = (iota((part, slots), 0) + (b * part + 1)).astype(F32)
            pick = jnp.where(target == place, scale, 0.0).astype(BF16)
            at = (pl.ds(b * part, part), pl.ds(half * cw, cw))
            out_ref[at] = out_ref[at] + (256.0 * dot(pick, high_in[...]) + dot(pick, low_in[...]))

    send_upper(0)
    send_lower(0)
    send_upper(1)
    index_rows()
    pass_upper(0)
    pass_lower(0)
    send_lower(1)
    send_upper(2)
    send_upper(3)
    build_hot(0)
    pass_upper(1)
    wait_lower(0)
    widen(0)
    schur_copy.wait()
    wait_upper(0)
    contribute(0)
    exchange(0)
    pass_upper(2)
    pass_lower(1)
    wait_upper(1)
    contribute(1)
    exchange(1)
    pass_upper(3)
    wait_lower(1)
    widen(1)
    build_hot(1)
    wait_upper(2)
    contribute(2)
    exchange(2)
    front_copy.wait()
    collect(0)
    wait_upper(3)
    contribute(3)
    exchange(3)
    collect(1)
    collect(2)
    collect(3)

    for step in range(2 * HALVES):
        sent = panel.at[step, pl.ds(0, (zs - 1) * depth), :]
        pltpu.make_async_remote_copy(
            src_ref=sent, dst_ref=sent, send_sem=z_send.at[step], recv_sem=z_recv.at[step, 0],
            device_id=(me, partner), device_id_type=MESH,
        ).wait_send()
        sent = panel.at[step, pl.ds(0, (X - 1) * zs * depth), :]
        pltpu.make_async_remote_copy(
            src_ref=sent, dst_ref=sent, send_sem=x_send.at[step], recv_sem=x_recv.at[step],
            device_id=(me, partner), device_id_type=MESH,
        ).wait_send()
        all_codes(step).wait_send()
        all_meta(step).wait_send()
    for child in range(2):
        sent = packed.at[child, pl.ds(0, ys - 1)]
        pltpu.make_async_remote_copy(
            src_ref=sent, dst_ref=sent, send_sem=y_send.at[child], recv_sem=y_recv.at[child, 0],
            device_id=(me, partner), device_id_type=MESH,
        ).wait_send()
        sent = packed.at[child, pl.ds(0, ys)]
        pltpu.make_async_remote_copy(
            src_ref=sent, dst_ref=sent, send_sem=c_send.at[child], recv_sem=c_recv.at[child],
            device_id=(me, partner), device_id_type=MESH,
        ).wait_send()


def shards(count, cols, schur, lower, upper, tile_mask, row_map, front):
    children, rows, _ = lower.shape
    width = schur.shape[2]
    depth = upper.shape[1]
    cap = 3 * rows // (2 * count)
    slots = count * cap
    cw = width // HALVES
    steps = children * HALVES
    full = depth * count
    zs = count // X
    ys = cols // CORES
    dims = (count, cols, rows, width, depth, cap)
    vmem = pl.BlockSpec(memory_space=pltpu.VMEM)
    hbm = pl.BlockSpec(memory_space=pl.ANY)
    dma = pltpu.SemaphoreType.DMA
    return pl.pallas_call(
        functools.partial(kernel, dims),
        out_shape=jax.ShapeDtypeStruct((rows, width), F32),
        in_specs=[vmem, vmem, pl.BlockSpec(memory_space=pltpu.SMEM), vmem, hbm, hbm],
        out_specs=vmem,
        scratch_shapes=[
            pltpu.VMEM((children, rows, width), F32),
            pltpu.VMEM((children, cols, rows + 16, TILE), BF16),
            pltpu.VMEM((rows, full), BF16),
            pltpu.VMEM((steps, full, cw), BF16),
            pltpu.VMEM((rows, rows), BF16),
            pltpu.VMEM((slots, rows), BF16),
            pltpu.VMEM((children, count, rows), BF16),
            pltpu.VMEM((8, rows), F32),
            pltpu.VMEM((rows, 8), F32),
            pltpu.VMEM((children, count, TILE), F32),
            pltpu.VMEM((rows, TILE), BF16),
            pltpu.VMEM((rows, cw), BF16),
            pltpu.VMEM((rows, cw), BF16),
            pltpu.VMEM((steps, slots, cw), jnp.int16),
            pltpu.VMEM((steps, slots, cw), jnp.int16),
            pltpu.VMEM((steps, count, 1, TILE), F32),
            pltpu.VMEM((steps, count, 1, TILE), F32),
            pltpu.VMEM((count, TILE), F32),
            pltpu.VMEM((2, TILE, slots), BF16),
            pltpu.VMEM((slots, cw), BF16),
            pltpu.VMEM((slots, cw), BF16),
            dma((14,)),
            dma((steps,)),
            dma((steps, zs)),
            dma((steps,)),
            dma((steps,)),
            dma((children,)),
            dma((children, ys)),
            dma((children,)),
            dma((children,)),
            dma((steps,)),
            dma((steps,)),
            dma((steps,)),
            dma((steps,)),
        ],
        compiler_params=pltpu.CompilerParams(
            collective_id=0, has_side_effects=True, vmem_limit_bytes=60 * 2**20
        ),
    )(lower, upper, tile_mask, row_map, schur, front)


def solution(mesh):
    count, cols = mesh.shape["row"], mesh.shape["col"]
    split = P(None, "row", "col")
    return jax.shard_map(
        functools.partial(shards, count, cols),
        mesh=mesh,
        in_specs=(split, split, split, split, P(None, "row"), P("row", "col")),
        out_specs=P("row", "col"),
        check_vma=False,
    )
```

time: 344 us -> 116 us (0.34)
  waiting for transfers between devices: 162 us -> 0 us
  Pallas kernels: 0 us -> 110 us
  local copies, waits for them, and re-layouts: 64.1 us -> 4.44 us
  other arithmetic: 44.3 us -> 0 us
  blocking collectives: 22.6 us -> 0 us
  starting transfers between devices: 21.6 us -> 0 us
  between operations: 13.7 us -> 0.01 us
  matrix products: 10.8 us -> 0 us
    all_to_all x2 -> x0, waiting for transfers between devices: 141 us -> none  [the longest x1 141 us: shards(): lax.all_to_all(values, ROW, split_axis=1, concat_axis=1, tiled=True)]
    pallas_call x0 -> x1, Pallas kernels: none -> 110 us  [shards(): pl.pallas_call(functools.partial(kernel, dims), out_shape=jax.ShapeDtypeS...]
    all_gather x2 -> x0, blocking collectives: 22.6 us -> none  [the longest x1 14 us: gathered_by_axis(): result = lax.all_gather(result, axes[number], axis=dim, tiled=True)]
    scatter-add x1 -> x0, other arithmetic: 22.1 us -> none  [assemble(): return result.at[index].add(values.reshape(-1, width), mode='drop')]
    all_to_all x2 -> x0, starting transfers between devices: 21.5 us -> none  [the longest x1 11.4 us: shards(): lax.all_to_all(places, ROW, split_axis=1, concat_axis=1, tiled=True)]
    unnamed x24 -> x2, local copies, waits for them, and re-layouts: 25.1 us -> 4.44 us
    all_gather x2 -> x0, waiting for transfers between devices: 20.6 us -> none  [the longest x1 20.6 us: shards(): lax.all_gather(packed, 'col', axis=2, tiled=True)]
    mul x4 -> x0, local copies, waits for them, and re-layouts: 19.7 us -> none  [shards(): packed_five * select[:, :, None, :, None]]
  transfers between devices with their start and end apart: 4 -> 0, of which waited for: 2 -> 0; matrix products, arithmetic and copies ran while one was open for 25% -> 0% of each run, Pallas kernels for 0% -> 0%
where the time goes in v1:
time: 116 us; the launch traced here: 115 us
  Pallas kernels  110 us (95%)
  local copies, waits for them, and re-layouts  4.44 us (4%)
    pallas_call x1, Pallas kernels, shards(): pl.pallas_call(functools.partial(kernel, dims), out_shape=jax.ShapeDtypeS...  110 us
    unnamed x2, local copies, waits for them, and re-layouts  4.44 us

profile of v1, /device:TPU:16, one launch (start us, length us, event | category | flops | bytes accessed | tf_op | source)
XLA Modules:
  0.0 114.6 jit_solution(2127590301820055728)
XLA Ops:
  0.0 1.4 %copy.7.mask_ref = s32[2,8,2]{2,1,0:T(8,128)} copy(s32[2,8,2]{1,2,0:T(2,128)} %param.9) | data formatting | bytes 256 | tf_op args[3]
  1.4 110.2 %shard_map.64 = f32[1024,512]{1,0:T(8,128)} custom-call(bf16[2,1024,256]{2,1,0:T(8,128)(2,1)} %lower_ref.1, bf16[2,64,512]{2,1,0:T(8,128)(2,1)} %upper_ref.1, s32[2,8,2]{2,1,0:T(8,128)} %copy.7.mask_ref, s32[2,1024]{1,0:T(2,128)} %map_ref.1, f32[2,1024,512]{2,1,0:T(8,128)} %schur_hbm.1, f32[1024,512]{1,0:T(8,128)} %front_hbm.1), custom_call_target="tpu_custom_call" | custom-call | tf_op jit(solution)/shard_map/pallas_call | solution.py:485
  111.5 3.1 %copy.9 = f32[1024,512]{1,0:T(8,128)} copy(f32[1024,512]{1,0:T(8,128)} %shard_map.64) | data formatting | bytes 4194304

commit v2 on v1

v2 whole, which is shorter than its diff:
```python
import functools

import jax
import jax.numpy as jnp
from jax import lax
from jax.experimental import pallas as pl
from jax.experimental.pallas import tpu as pltpu
from jax.sharding import PartitionSpec as P

TILE = 128
X = 4
CORES = 2
STEPS = ((0, 0, 1), (0, 1, 1), (0, 2, 2), (1, 0, 2), (1, 2, 2))
DIRECT = 2
GROUPS = 2
MESH = pl.DeviceIdType.MESH
F32 = jnp.float32
BF16 = jnp.bfloat16
I32 = jnp.int32


def dot(a, b):
    return jnp.dot(a, b, preferred_element_type=F32)


def iota(shape, dim):
    return lax.broadcasted_iota(I32, shape, dim)


def kernel(
    dims,
    lower_hbm,
    upper_hbm,
    mask_ref,
    map_ref,
    schur_hbm,
    out_ref,
    s,
):
    count, cols, rows, width, depth, cap = dims
    zs = count // X
    ys = cols // CORES
    quarter = width // 4
    slots = count * cap
    steps = len(STEPS)
    members = count // GROUPS
    me = lax.axis_index("row")
    col = lax.axis_index("col")
    my_z = me // X
    my_x = lax.rem(me, X)
    my_y = col // CORES
    core = lax.rem(col, CORES)
    partner = my_y * CORES + (1 - core)
    lower, upper, schur, packed, wide, panel = s["lower"], s["upper"], s["schur"], s["packed"], s["wide"], s["panel"]
    square, hot, owner = s["square"], s["hot"], s["owner"]
    rows_info, cols_info, place_info = s["rows_info"], s["cols_info"], s["place_info"]
    scale_col, high, low = s["scale_col"], s["high"], s["low"]
    code_out, code_in, meta_out, meta_in = s["code_out"], s["code_in"], s["meta_out"], s["meta_in"]
    meta_flat, spread, high_in, low_in = s["meta_flat"], s["spread"], s["high_in"], s["low_in"]
    local_sem = s["local_sem"]

    barrier = pltpu.get_barrier_semaphore()

    def greet_row(k, carry):
        pl.semaphore_signal(barrier, inc=1, device_id=(lax.rem(me + k, count), col), device_id_type=MESH)
        return carry

    def greet_col(k, carry):
        pl.semaphore_signal(barrier, inc=1, device_id=(me, lax.rem(col + k, cols)), device_id_type=MESH)
        return carry

    lax.fori_loop(1, count, greet_row, 0)
    lax.fori_loop(1, cols, greet_col, 0)

    lower_copy = pltpu.make_async_copy(lower_hbm, lower, local_sem.at[1])
    upper_copy = pltpu.make_async_copy(upper_hbm, upper, local_sem.at[2])
    schur_copy = pltpu.make_async_copy(schur_hbm, schur, local_sem.at[0])
    lower_copy.start()
    upper_copy.start()
    schur_copy.start()

    def remote(source, target, sent, got, device):
        return pltpu.make_async_remote_copy(
            src_ref=source, dst_ref=target, send_sem=sent, recv_sem=got, device_id=device, device_id_type=MESH
        )

    def total(ref, sent, got):
        return remote(ref, ref, sent, got, (me, partner))

    def pack(child):
        for tile in range(rows // TILE):
            at = pl.ds(tile * TILE, TILE)
            second = mask_ref[child, 1, tile]
            packed[child, col, at, :] = jnp.where(
                second == 1, lower[child, at, TILE : 2 * TILE], lower[child, at, 0:TILE]
            )
        row = iota((16, TILE), 0)
        flags = jnp.zeros((16, TILE), F32)
        for tile in range(rows // TILE):
            flags = jnp.where(row == tile, mask_ref[child, 1, tile].astype(F32), flags)
        packed[child, col, pl.ds(rows, 16), :] = flags.astype(BF16)

    def upper_block(step):
        child, first, number = STEPS[step]
        return upper.at[child, :, pl.ds(first * quarter, number * quarter)]

    def panel_block(step, z, x):
        start = pl.multiple_of((z * X + x) * depth, depth)
        return panel[step].at[pl.ds(start, depth), :]

    def nearest(n):
        half = n // 2 + 1
        return half + lax.rem(n, 2) * (zs - 2 * half)

    def z_copy(step, dz):
        z = lax.rem(my_z + dz, zs)
        return remote(
            upper_block(step),
            panel_block(step, my_z, my_x),
            s["z_send"].at[step],
            s["z_recv"].at[step, dz],
            (z * X + my_x, col),
        )

    def x_copy(step, source, z, dx):
        return remote(
            source,
            panel_block(step, z, my_x),
            s["x_send"].at[step],
            s["x_recv"].at[step],
            (my_z * X + lax.rem(my_x + dx, X), col),
        )

    def send_own(step):
        for dx in (1, 3, 2):
            x_copy(step, upper_block(step), my_z, dx).start()
        pltpu.make_async_copy(upper_block(step), panel_block(step, my_z, my_x), local_sem.at[3 + step]).start()

    def send_upper(step):
        def body(n, carry):
            z_copy(step, nearest(n)).start()
            return carry

        lax.fori_loop(0, zs - 1, body, 0)
        send_own(step)

    def pass_upper(step):
        def body(n, carry):
            dz = nearest(n)
            z_copy(step, dz).wait_recv()
            z = lax.rem(my_z - dz + zs, zs)
            for dx in (1, 3, 2):
                x_copy(step, panel_block(step, z, my_x), z, dx).start()
            return carry

        lax.fori_loop(0, zs - 1, body, 0)

    def reach(step, way):
        return zs // 2 if (step % 2 == 0) == (way > 0) else zs // 2 - 1

    def hop_copy(step, way, hop):
        z = lax.rem(my_z - way * (hop - 1) + zs, zs)
        block = upper_block(step) if hop == 1 else panel_block(step, z, my_x)
        return remote(
            block,
            panel_block(step, z, my_x),
            s["z_send"].at[step],
            s["z_recv"].at[step, (way * hop) % zs],
            (lax.rem(my_z + way + zs, zs) * X + my_x, col),
        )

    def hop_wait(step, hop):
        for way in (1, -1):
            if hop <= reach(step, way):
                hop_copy(step, way, hop).wait_recv()

    def hop_send(step, hop):
        for way in (1, -1):
            if hop <= reach(step, way):
                hop_copy(step, way, hop).start()

    def hops(hop):
        for step in range(DIRECT, steps):
            hop_wait(step, hop)
            hop_send(step, hop + 1)

    def x_spread(step):
        send_own(step)

        def body(n, carry):
            z = lax.rem(my_z + n, zs)
            for dx in (1, 3, 2):
                x_copy(step, panel_block(step, z, my_x), z, dx).start()
            return carry

        lax.fori_loop(1, zs, body, 0)

    def all_x(step):
        return total(
            panel[step].at[pl.ds(0, (X - 1) * zs * depth), :], s["x_send"].at[step], s["x_recv"].at[step]
        )

    def wait_upper(step):
        pltpu.make_async_copy(upper_block(step), panel_block(step, my_z, my_x), local_sem.at[3 + step]).wait()
        all_x(step).wait_recv()

    middle = rows // 2
    parts = (pl.ds(0, middle), pl.ds(middle, rows + 16 - middle))

    def y_copy(child, way, part, hop):
        block = lax.rem(my_y - way * (hop - 1) + ys, ys) * CORES + core
        ref = packed.at[child, block, parts[part], :]
        return remote(
            ref,
            ref,
            s["y_send"].at[child, (1 + way) // 2, part, hop - 1],
            s["y_recv"].at[child, (1 + way) // 2, part, hop - 1],
            (me, lax.rem(my_y + way + ys, ys) * CORES + core),
        )

    def c_copy(child, behind, part):
        block = lax.rem(my_y - behind + ys, ys) * CORES + core
        ref = packed.at[child, block, parts[part], :]
        return remote(ref, ref, s["c_send"].at[child], s["c_recv"].at[child], (me, partner))

    def send_lower(child):
        for way, part in ((1, 0), (-1, 1), (1, 1), (-1, 0)):
            y_copy(child, way, part, 1).start()
        for part in range(2):
            c_copy(child, 0, part).start()

    def pass_lower(child):
        for way, part in ((1, 0), (-1, 1)):
            y_copy(child, way, part, 1).wait_recv()
            y_copy(child, way, part, 2).start()
            c_copy(child, way, part).start()

    def pass_lower_again(child):
        for way, part in ((1, 1), (-1, 0)):
            y_copy(child, way, part, 1).wait_recv()
            c_copy(child, way, part).start()
        for way, part in ((1, 0), (-1, 1)):
            y_copy(child, way, part, 2).wait_recv()
            c_copy(child, 2 * way, part).start()

    def all_c(child):
        return total(packed.at[child, pl.ds(0, ys)], s["c_send"].at[child], s["c_recv"].at[child])

    def index_rows():
        def strict(b, carry):
            at = pl.ds(pl.multiple_of(b * TILE, TILE), TILE)
            before = iota((TILE, rows), 0) + b * TILE < iota((TILE, rows), 1)
            square[at, :] = jnp.where(before, 1.0, 0.0).astype(BF16)
            return carry

        lax.fori_loop(0, rows // TILE, strict, 0)
        for child in range(2):
            line = map_ref[pl.ds(child, 1), :]
            same = iota((count, rows), 0) == line // rows
            owner[child] = jnp.where(same, 1.0, 0.0).astype(BF16)
        rows_info[...] = jnp.zeros_like(rows_info)
        for child in range(2):
            line = map_ref[pl.ds(child, 1), :]
            hits = owner[child]
            ahead = dot(hits, square[...])
            rank = jnp.sum(ahead * hits.astype(F32), axis=0, keepdims=True)
            spot = lax.rem(line, rows) + 1
            rows_info[pl.ds(4 * child, 1), :] = rank
            rows_info[pl.ds(4 * child + 1, 1), :] = (spot // 32).astype(F32)
            rows_info[pl.ds(4 * child + 2, 1), :] = lax.rem(spot, 32).astype(F32)
            rows_info[pl.ds(4 * child + 3, 1), :] = (line // rows).astype(F32)

        def identity(b, carry):
            at = pl.ds(pl.multiple_of(b * TILE, TILE), TILE)
            equal = iota((TILE, rows), 0) + b * TILE == iota((TILE, rows), 1)
            square[at, :] = jnp.where(equal, 1.0, 0.0).astype(BF16)
            return carry

        lax.fori_loop(0, rows // TILE, identity, 0)
        cols_info[...] = lax.dot_general(
            square[...], rows_info[...].astype(BF16), (((1,), (1,)), ((), ())), preferred_element_type=F32
        )
        for child in range(2):
            lane = iota((rows, TILE), 1).astype(F32)
            match = lane - 64.0 == cols_info[:, 4 * child : 4 * child + 1]
            tops = jnp.where(match, cols_info[:, 4 * child + 1 : 4 * child + 2], 0.0).astype(BF16)
            ends = jnp.where(match, cols_info[:, 4 * child + 2 : 4 * child + 3], 0.0).astype(BF16)
            place_info[child] = 32.0 * dot(owner[child], tops) + dot(owner[child], ends)
        slot = iota((TILE, members * cap), 1).astype(F32)
        inner = slot - cap * jnp.floor((slot + 0.5) * (1.0 / cap))
        lane = iota((TILE, members * cap), 0).astype(F32)
        spread[0] = jnp.where(lane == inner, 1.0, 0.0).astype(BF16)
        spread[1] = jnp.where(lane - 64.0 == inner, 1.0, 0.0).astype(BF16)

    def build_hot(child):
        flat = rows_info[pl.ds(4 * child + 3, 1), :] * float(cap) + rows_info[pl.ds(4 * child, 1), :]

        def body(b, carry):
            at = pl.ds(pl.multiple_of(b * TILE, TILE), TILE)
            slot = (iota((TILE, rows), 0) + b * TILE).astype(F32)
            hot[at, :] = jnp.where(slot == flat, 1.0, 0.0).astype(BF16)
            return carry

        lax.fori_loop(0, slots // TILE, body, 0)

    def widen(child):
        def body(j, carry):
            flags = packed[child, j, pl.ds(rows, 16), :].astype(F32)
            for tile in range(rows // TILE):
                at = pl.ds(tile * TILE, TILE)
                block = packed[child, j, at, :].astype(F32)
                flag = flags[tile : tile + 1, :]
                left = pl.multiple_of(j * 2 * TILE, TILE)
                right = pl.multiple_of(j * 2 * TILE + TILE, TILE)
                wide[at, pl.ds(left, TILE)] = (block * (1.0 - flag)).astype(BF16)
                wide[at, pl.ds(right, TILE)] = (block * flag).astype(BF16)
            return carry

        lax.fori_loop(0, cols, body, 0)

    def contribute(step):
        child, first, number = STEPS[step]
        cw = number * quarter
        part = rows // 2
        for b in range(2):
            at = pl.ds(b * part, part)
            update = dot(wide[at, :], panel[step][...])
            value = schur[child, at, pl.ds(first * quarter, cw)] - update
            peak = jnp.maximum(jnp.max(jnp.abs(value), axis=1, keepdims=True), 1e-30)
            scale_col[at, :] = jnp.broadcast_to(peak * ((1.0 + 2.0**-8) / 32767.0), (part, TILE)).astype(BF16)
            inverse = 1.0 / scale_col[at, :].astype(F32)
            code = jnp.floor(value * inverse[:, 0:1] + 0.5)
            top = jnp.floor(code * (1.0 / 256.0))
            high[at, 0:cw] = top.astype(BF16)
            low[at, 0:cw] = (code - 256.0 * top).astype(BF16)
        size = slots // 3
        for b in range(3):
            at = pl.ds(b * size, size)
            code = 256.0 * dot(hot[at, :], high[:, 0:cw]) + dot(hot[at, :], low[:, 0:cw])
            code_out[step][at, :] = code.astype(I32).astype(jnp.int16)
        lane = iota((rows, TILE), 1).astype(F32)
        match = lane == cols_info[:, 4 * child : 4 * child + 1]
        scales = jnp.where(match, scale_col[...].astype(F32), 0.0).astype(BF16)
        meta = dot(owner[child], scales) + place_info[child]
        for t in range(count):
            meta_out[step, t] = meta[t : t + 1, :]

    def rows_of(t):
        return pl.ds(pl.multiple_of(t * cap, 16), cap)

    def shift(n):
        place = n // 2 + lax.rem(n, 2) * (count - 2 - 2 * (n // 2))
        half = place // 2 + 1
        return half + lax.rem(place, 2) * (count - 2 * half)

    def e_copy(step, n, group):
        t = lax.rem(me + shift(n), count)
        return remote(
            code_out[step].at[rows_of(t), :],
            code_in[step].at[rows_of(n), :],
            s["e_send"].at[step],
            s["e_recv"].at[step, group],
            (t, col),
        )

    def m_copy(step, n, group):
        t = lax.rem(me + shift(n), count)
        return remote(
            meta_out.at[step, t], meta_in.at[step, n], s["m_send"].at[step], s["m_recv"].at[step, group], (t, col)
        )

    def own_copies(step):
        return (
            pltpu.make_async_copy(
                code_out[step].at[rows_of(me), :], code_in[step].at[rows_of(count - 1), :], local_sem.at[8 + step]
            ),
            pltpu.make_async_copy(meta_out.at[step, me], meta_in.at[step, count - 1], local_sem.at[13 + step]),
        )

    def exchange(step):
        for group in range(GROUPS):

            def body(n, carry):
                m_copy(step, n, group).start()
                e_copy(step, n, group).start()
                return carry

            lax.fori_loop(group * members, min((group + 1) * members, count - 1), body, 0)
        for copy in own_copies(step):
            copy.start()

    def all_codes(step, group, number):
        ref = code_in[step].at[pl.ds(0, number * cap), :]
        return total(ref, s["e_send"].at[step], s["e_recv"].at[step, group])

    def all_meta(step, group, number):
        ref = meta_in.at[step, pl.ds(0, number)]
        return total(ref, s["m_send"].at[step], s["m_recv"].at[step, group])

    def collect(step, group):
        _, first, number = STEPS[step]
        cw = number * quarter
        others = members
        if group == GROUPS - 1:
            others = members - 1
            for copy in own_copies(step):
                copy.wait()
        all_meta(step, group, others).wait_recv()
        for m in range(members):
            meta_flat[m : m + 1, :] = meta_in[step, group * members + m]
        flat = meta_flat[...]
        tops = jnp.floor(flat * (1.0 / 32.0))
        ends = flat - 32.0 * tops
        places = 32.0 * dot(tops.astype(BF16), spread[1]) + dot(ends.astype(BF16), spread[1])
        scales = dot(flat.astype(BF16), spread[0])
        size = members * cap
        slot = iota((members, size), 1)
        start = iota((members, size), 0) * cap
        own = (slot >= start) & (slot < start + cap)
        place = jnp.sum(jnp.where(own, places, 0.0), axis=0, keepdims=True)
        scale = jnp.sum(jnp.where(own, scales, 0.0), axis=0, keepdims=True)
        all_codes(step, group, others).wait_recv()
        code = code_in[step][group * size : (group + 1) * size, :].astype(I32)
        high_in[:, 0:cw] = (code >> 8).astype(F32).astype(BF16)
        low_in[:, 0:cw] = (code & 255).astype(F32).astype(BF16)
        part = rows // 2
        for b in range(2):
            target = (iota((part, size), 0) + (b * part + 1)).astype(F32)
            pick = jnp.where(target == place, scale, 0.0).astype(BF16)
            at = (pl.ds(b * part, part), pl.ds(first * quarter, cw))
            value = 256.0 * dot(pick, high_in[:, 0:cw]) + dot(pick, low_in[:, 0:cw])
            if STEPS[step][0] == 0 and group == 0:
                out_ref[at] = value
            else:
                out_ref[at] = out_ref[at] + value

    lower_copy.wait()
    upper_copy.wait()
    pack(0)
    pl.semaphore_wait(barrier, count + cols - 2)
    send_upper(0)
    send_lower(0)
    send_upper(1)
    for step in range(DIRECT, steps):
        hop_send(step, 1)
    pack(1)
    index_rows()
    pass_upper(0)
    pass_lower(0)
    pass_upper(1)
    hops(1)
    pass_lower_again(0)
    send_lower(1)
    build_hot(0)
    hops(2)
    all_c(0).wait_recv()
    widen(0)
    schur_copy.wait()
    hops(3)
    wait_upper(0)
    contribute(0)
    exchange(0)
    for step in range(DIRECT, steps):
        hop_wait(step, 4)
    x_spread(2)
    pass_lower(1)
    wait_upper(1)
    contribute(1)
    exchange(1)
    x_spread(3)
    pass_lower_again(1)
    wait_upper(2)
    contribute(2)
    exchange(2)
    x_spread(4)
    all_c(1).wait_recv()
    widen(1)
    build_hot(1)
    collect(0, 0)
    collect(0, 1)
    wait_upper(3)
    contribute(3)
    exchange(3)
    collect(1, 0)
    collect(1, 1)
    wait_upper(4)
    contribute(4)
    exchange(4)
    for step in range(2, steps):
        for group in range(GROUPS):
            collect(step, group)

    for step in range(steps):
        total(
            panel[step].at[pl.ds(0, (zs - 1) * depth), :], s["z_send"].at[step], s["z_recv"].at[step, 0]
        ).wait_send()
        all_x(step).wait_send()
        all_codes(step, 0, count - 1).wait_send()
        all_meta(step, 0, count - 1).wait_send()
    for child in range(2):
        for part in range(2):
            for way in (1, -1):
                y_copy(child, way, part, 1).wait_send()
            y_copy(child, 1 - 2 * part, part, 2).wait_send()
        all_c(child).wait_send()


def shards(count, cols, schur, lower, upper, tile_mask, row_map, front):
    children, rows, _ = lower.shape
    width = schur.shape[2]
    depth = upper.shape[1]
    cap = 3 * rows // (2 * count)
    slots = count * cap
    steps = len(STEPS)
    full = depth * count
    zs = count // X
    members = count // GROUPS
    dims = (count, cols, rows, width, depth, cap)
    widths = [width // 4 * number for _, _, number in STEPS]
    half = width // 2
    vmem = pl.BlockSpec(memory_space=pltpu.VMEM)
    hbm = pl.BlockSpec(memory_space=pltpu.HBM)
    dma = pltpu.SemaphoreType.DMA
    scratch = dict(
        lower=pltpu.VMEM(lower.shape, BF16),
        upper=pltpu.VMEM(upper.shape, BF16),
        schur=pltpu.VMEM(schur.shape, F32),
        packed=pltpu.VMEM((children, cols, rows + 16, TILE), BF16),
        wide=pltpu.VMEM((rows, full), BF16),
        panel=[pltpu.VMEM((full, w), BF16) for w in widths],
        square=pltpu.VMEM((rows, rows), BF16),
        hot=pltpu.VMEM((slots, rows), BF16),
        owner=pltpu.VMEM((children, count, rows), BF16),
        rows_info=pltpu.VMEM((8, rows), F32),
        cols_info=pltpu.VMEM((rows, 8), F32),
        place_info=pltpu.VMEM((children, count, TILE), F32),
        scale_col=pltpu.VMEM((rows, TILE), BF16),
        high=pltpu.VMEM((rows, half), BF16),
        low=pltpu.VMEM((rows, half), BF16),
        code_out=[pltpu.VMEM((slots, w), jnp.int16) for w in widths],
        code_in=[pltpu.VMEM((slots, w), jnp.int16) for w in widths],
        meta_out=pltpu.VMEM((steps, count, 1, TILE), F32),
        meta_in=pltpu.VMEM((steps, count, 1, TILE), F32),
        meta_flat=pltpu.VMEM((members, TILE), F32),
        spread=pltpu.VMEM((2, TILE, members * cap), BF16),
        high_in=pltpu.VMEM((members * cap, half), BF16),
        low_in=pltpu.VMEM((members * cap, half), BF16),
        local_sem=dma((18,)),
        z_send=dma((steps,)),
        z_recv=dma((steps, zs)),
        x_send=dma((steps,)),
        x_recv=dma((steps,)),
        y_send=dma((children, 2, 2, 2)),
        y_recv=dma((children, 2, 2, 2)),
        c_send=dma((children,)),
        c_recv=dma((children,)),
        e_send=dma((steps,)),
        e_recv=dma((steps, GROUPS)),
        m_send=dma((steps,)),
        m_recv=dma((steps, GROUPS)),
    )
    added = pl.pallas_call(
        functools.partial(kernel, dims),
        out_shape=jax.ShapeDtypeStruct((rows, width), F32),
        in_specs=[hbm, hbm, pl.BlockSpec(memory_space=pltpu.SMEM), vmem, hbm],
        out_specs=vmem,
        scratch_shapes=[scratch],
        compiler_params=pltpu.CompilerParams(
            collective_id=0, has_side_effects=True, vmem_limit_bytes=50 * 2**20
        ),
    )(lower, upper, jnp.swapaxes(tile_mask, 1, 2), row_map, schur)
    return front + added


def solution(mesh):
    count, cols = mesh.shape["row"], mesh.shape["col"]
    split = P(None, "row", "col")
    return jax.shard_map(
        functools.partial(shards, count, cols),
        mesh=mesh,
        in_specs=(split, split, split, split, P(None, "row"), P("row", "col")),
        out_specs=P("row", "col"),
        check_vma=False,
    )
```

time: 116 us -> 124 us (1.069)
  Pallas kernels: 110 us -> 118 us
  other arithmetic: 0 us -> 1.8 us
    pallas_call x1, Pallas kernels: 110 us -> 118 us  [shards(): pl.pallas_call(functools.partial(kernel, dims), out_shape=jax.ShapeDtypeS...]
    add x0 -> x1, other arithmetic: none -> 1.8 us  [shards(): return front + added]
    unnamed x2 -> x10, local copies, waits for them, and re-layouts: 4.44 us -> 3.51 us
where the time goes in v2:
time: 124 us; the launch traced here: 123 us
  Pallas kernels  118 us (95%)
  local copies, waits for them, and re-layouts  3.51 us (3%)
  other arithmetic  1.8 us (1%)
    pallas_call x1, Pallas kernels, shards(): pl.pallas_call(functools.partial(kernel, dims), out_shape=jax.ShapeDtypeS...  118 us
    unnamed x10, local copies, waits for them, and re-layouts  3.51 us

profile of v2, /device:TPU:16, one launch (start us, length us, event | category | flops | bytes accessed | tf_op | source)
XLA Modules:
  0.0 123.0 jit_solution(13952610522760383247)
XLA Ops:
  0.0 0.0 copy-start
  0.0 1.2 copy-done
  1.2 0.0 copy-start.1
  1.2 0.9 copy-done.1
  2.1 0.0 copy-start.2
  2.1 0.7 copy-done.2
  2.8 0.0 copy-start.3
  2.8 0.7 copy-done.3
  3.5 0.0 copy-start.4
  3.5 117.6 %shard_map.64 = f32[1024,512]{1,0:T(8,128)S(1)} custom-call(bf16[2,1024,256]{2,1,0:T(8,128)(2,1)S(1)} %copy-done, bf16[2,64,512]{2,1,0:T(8,128)(2,1)S(1)} %copy-done.1, s32[2,2,8]{2,1,0:T(2,128)S(1)} %bitcast.1, s32[2,1024]{1,0:T(2,128)S(1)} %copy-done.2, f32[2,1024,512]{2,1,0:T(8,128)} %schur_hbm.1), custom_call_target="tpu_custom_call" | custom-call | tf_op jit(solution)/shard_map/pallas_call | solution.py:562
  121.2 0.0 copy-done.4
  121.2 1.8 %add.3 = f32[1024,512]{1,0:T(8,128)} add(f32[1024,512]{1,0:T(8,128)S(1)} %copy-done.4, f32[1024,512]{1,0:T(8,128)S(1)} %shard_map.64) | non-fusion elementwise | flops 524288 | bytes 6291456 | tf_op jit(solution)/shard_map/add | solution.py:572
Async XLA Ops:
  0.0 1.2 copy-start
  1.2 0.9 copy-start.1
  2.1 0.7 copy-start.2
  2.8 0.7 copy-start.3
  3.5 117.6 %copy-start.4 = (f32[1024,512]{1,0:T(8,128)S(1)}, f32[1024,512]{1,0:T(8,128)}, u32[]{:S(2)}) copy-start(f32[1024,512]{1,0:T(8,128)} %param.11) | copy-start | bytes 6291460

commit v3 on v2

--- a/solution.py
+++ b/solution.py
@@ -12,7 +12,7 @@
 CORES = 2
 STEPS = ((0, 0, 1), (0, 1, 1), (0, 2, 2), (1, 0, 2), (1, 2, 2))
 DIRECT = 2
-GROUPS = 2
+GROUPS = (1, 1, 1, 1, 4)
 MESH = pl.DeviceIdType.MESH
 F32 = jnp.float32
 BF16 = jnp.bfloat16
@@ -43,7 +43,6 @@
     quarter = width // 4
     slots = count * cap
     steps = len(STEPS)
-    members = count // GROUPS
     me = lax.axis_index("row")
     col = lax.axis_index("col")
     my_z = me // X
@@ -54,9 +53,9 @@
     lower, upper, schur, packed, wide, panel = s["lower"], s["upper"], s["schur"], s["packed"], s["wide"], s["panel"]
     square, hot, owner = s["square"], s["hot"], s["owner"]
     rows_info, cols_info, place_info = s["rows_info"], s["cols_info"], s["place_info"]
-    scale_col, high, low = s["scale_col"], s["high"], s["low"]
+    scale_col, both, both_in = s["scale_col"], s["both"], s["both_in"]
     code_out, code_in, meta_out, meta_in = s["code_out"], s["code_in"], s["meta_out"], s["meta_in"]
-    meta_flat, spread, high_in, low_in = s["meta_flat"], s["spread"], s["high_in"], s["low_in"]
+    meta_flat, spread = s["meta_flat"], s["spread"]
     local_sem = s["local_sem"]
 
     barrier = pltpu.get_barrier_semaphore()
@@ -122,18 +121,33 @@
             (z * X + my_x, col),
         )
 
-    def x_copy(step, source, z, dx):
+    def behind(i):
+        return nearest(i - 1) if i else 0
+
+    def x_copy(step, i, way):
+        z = lax.rem(my_z - behind(i) + zs, zs)
         return remote(
-            source,
+            upper_block(step) if i == 0 else panel_block(step, z, my_x),
             panel_block(step, z, my_x),
             s["x_send"].at[step],
-            s["x_recv"].at[step],
-            (my_z * X + lax.rem(my_x + dx, X), col),
+            s["x_recv"].at[step, (1 + way) // 2, i % 2],
+            (my_z * X + lax.rem(my_x + way + X, X), col),
+        )
+
+    def far_copy(step, i, way):
+        z = lax.rem(my_z - behind(i) + zs, zs)
+        block = panel_block(step, z, lax.rem(my_x - way + X, X))
+        return remote(
+            block,
+            block,
+            s["x_send"].at[step],
+            s["far_recv"].at[step],
+            (my_z * X + lax.rem(my_x + way + X, X), col),
         )
 
     def send_own(step):
-        for dx in (1, 3, 2):
-            x_copy(step, upper_block(step), my_z, dx).start()
+        for way in (1, -1):
+            x_copy(step, 0, way).start()
         pltpu.make_async_copy(upper_block(step), panel_block(step, my_z, my_x), local_sem.at[3 + step]).start()
 
     def send_upper(step):
@@ -145,15 +159,23 @@
         send_own(step)
 
     def pass_upper(step):
-        def body(n, carry):
-            dz = nearest(n)
-            z_copy(step, dz).wait_recv()
-            z = lax.rem(my_z - dz + zs, zs)
-            for dx in (1, 3, 2):
-                x_copy(step, panel_block(step, z, my_x), z, dx).start()
-            return carry
-
-        lax.fori_loop(0, zs - 1, body, 0)
+        for i in range(1, zs):
+            z_copy(step, behind(i)).wait_recv()
+            for way in (1, -1):
+                x_copy(step, i, way).start()
+
+    def near_x(step, way, part):
+        return total(
+            panel[step].at[pl.ds(0, zs // 2 * depth), :],
+            s["x_send"].at[step],
+            s["x_recv"].at[step, (1 + way) // 2, part],
+        )
+
+    def x_far(step):
+        for way, part in ((1, 0), (-1, 1)):
+            near_x(step, way, part).wait_recv()
+            for i in range(part, zs, 2):
+                far_copy(step, i, way).start()
 
     def reach(step, way):
         return zs // 2 if (step % 2 == 0) == (way > 0) else zs // 2 - 1
@@ -186,23 +208,22 @@
 
     def x_spread(step):
         send_own(step)
-
-        def body(n, carry):
-            z = lax.rem(my_z + n, zs)
-            for dx in (1, 3, 2):
-                x_copy(step, panel_block(step, z, my_x), z, dx).start()
-            return carry
-
-        lax.fori_loop(1, zs, body, 0)
+        for i in range(1, zs):
+            for way in (1, -1):
+                x_copy(step, i, way).start()
 
     def all_x(step):
         return total(
-            panel[step].at[pl.ds(0, (X - 1) * zs * depth), :], s["x_send"].at[step], s["x_recv"].at[step]
+            panel[step].at[pl.ds(0, (X - 1) * zs * depth), :], s["x_send"].at[step], s["far_recv"].at[step]
         )
 
     def wait_upper(step):
         pltpu.make_async_copy(upper_block(step), panel_block(step, my_z, my_x), local_sem.at[3 + step]).wait()
-        all_x(step).wait_recv()
+        near_x(step, 1, 1).wait_recv()
+        near_x(step, -1, 0).wait_recv()
+        total(
+            panel[step].at[pl.ds(0, zs * depth), :], s["x_send"].at[step], s["far_recv"].at[step]
+        ).wait_recv()
 
     middle = rows // 2
     parts = (pl.ds(0, middle), pl.ds(middle, rows + 16 - middle))
@@ -270,6 +291,7 @@
             rows_info[pl.ds(4 * child + 2, 1), :] = lax.rem(spot, 32).astype(F32)
             rows_info[pl.ds(4 * child + 3, 1), :] = (line // rows).astype(F32)
 
+    def index_cols():
         def identity(b, carry):
             at = pl.ds(pl.multiple_of(b * TILE, TILE), TILE)
             equal = iota((TILE, rows), 0) + b * TILE == iota((TILE, rows), 1)
@@ -286,9 +308,9 @@
             tops = jnp.where(match, cols_info[:, 4 * child + 1 : 4 * child + 2], 0.0).astype(BF16)
             ends = jnp.where(match, cols_info[:, 4 * child + 2 : 4 * child + 3], 0.0).astype(BF16)
             place_info[child] = 32.0 * dot(owner[child], tops) + dot(owner[child], ends)
-        slot = iota((TILE, members * cap), 1).astype(F32)
+        slot = iota((TILE, slots), 1).astype(F32)
         inner = slot - cap * jnp.floor((slot + 0.5) * (1.0 / cap))
-        lane = iota((TILE, members * cap), 0).astype(F32)
+        lane = iota((TILE, slots), 0).astype(F32)
         spread[0] = jnp.where(lane == inner, 1.0, 0.0).astype(BF16)
         spread[1] = jnp.where(lane - 64.0 == inner, 1.0, 0.0).astype(BF16)
 
@@ -331,12 +353,13 @@
             inverse = 1.0 / scale_col[at, :].astype(F32)
             code = jnp.floor(value * inverse[:, 0:1] + 0.5)
             top = jnp.floor(code * (1.0 / 256.0))
-            high[at, 0:cw] = top.astype(BF16)
-            low[at, 0:cw] = (code - 256.0 * top).astype(BF16)
+            both[at, 0:cw] = top.astype(BF16)
+            both[at, cw : 2 * cw] = (code - 256.0 * top).astype(BF16)
         size = slots // 3
         for b in range(3):
             at = pl.ds(b * size, size)
-            code = 256.0 * dot(hot[at, :], high[:, 0:cw]) + dot(hot[at, :], low[:, 0:cw])
+            moved = dot(hot[at, :], both[:, 0 : 2 * cw])
+            code = 256.0 * moved[:, 0:cw] + moved[:, cw : 2 * cw]
             code_out[step][at, :] = code.astype(I32).astype(jnp.int16)
         lane = iota((rows, TILE), 1).astype(F32)
         match = lane == cols_info[:, 4 * child : 4 * child + 1]
@@ -378,7 +401,8 @@
         )
 
     def exchange(step):
-        for group in range(GROUPS):
+        members = count // GROUPS[step]
+        for group in range(GROUPS[step]):
 
             def body(n, carry):
                 m_copy(step, n, group).start()
@@ -400,20 +424,22 @@
     def collect(step, group):
         _, first, number = STEPS[step]
         cw = number * quarter
+        members = count // GROUPS[step]
         others = members
-        if group == GROUPS - 1:
+        if group == GROUPS[step] - 1:
             others = members - 1
             for copy in own_copies(step):
                 copy.wait()
         all_meta(step, group, others).wait_recv()
         for m in range(members):
             meta_flat[m : m + 1, :] = meta_in[step, group * members + m]
-        flat = meta_flat[...]
+        flat = meta_flat[0:members, :]
         tops = jnp.floor(flat * (1.0 / 32.0))
         ends = flat - 32.0 * tops
-        places = 32.0 * dot(tops.astype(BF16), spread[1]) + dot(ends.astype(BF16), spread[1])
-        scales = dot(flat.astype(BF16), spread[0])
         size = members * cap
+        for_place, for_scale = spread[1, :, 0:size], spread[0, :, 0:size]
+        places = 32.0 * dot(tops.astype(BF16), for_place) + dot(ends.astype(BF16), for_place)
+        scales = dot(flat.astype(BF16), for_scale)
         slot = iota((members, size), 1)
         start = iota((members, size), 0) * cap
         own = (slot >= start) & (slot < start + cap)
@@ -421,14 +447,15 @@
         scale = jnp.sum(jnp.where(own, scales, 0.0), axis=0, keepdims=True)
         all_codes(step, group, others).wait_recv()
         code = code_in[step][group * size : (group + 1) * size, :].astype(I32)
-        high_in[:, 0:cw] = (code >> 8).astype(F32).astype(BF16)
-        low_in[:, 0:cw] = (code & 255).astype(F32).astype(BF16)
+        both_in[0:size, 0:cw] = (code >> 8).astype(F32).astype(BF16)
+        both_in[0:size, cw : 2 * cw] = (code & 255).astype(F32).astype(BF16)
         part = rows // 2
         for b in range(2):
             target = (iota((part, size), 0) + (b * part + 1)).astype(F32)
             pick = jnp.where(target == place, scale, 0.0).astype(BF16)
             at = (pl.ds(b * part, part), pl.ds(first * quarter, cw))
-            value = 256.0 * dot(pick, high_in[:, 0:cw]) + dot(pick, low_in[:, 0:cw])
+            moved = dot(pick, both_in[0:size, 0 : 2 * cw])
+            value = 256.0 * moved[:, 0:cw] + moved[:, cw : 2 * cw]
             if STEPS[step][0] == 0 and group == 0:
                 out_ref[at] = value
             else:
@@ -437,6 +464,7 @@
     lower_copy.wait()
     upper_copy.wait()
     pack(0)
+    index_rows()
     pl.semaphore_wait(barrier, count + cols - 2)
     send_upper(0)
     send_lower(0)
@@ -444,50 +472,53 @@
     for step in range(DIRECT, steps):
         hop_send(step, 1)
     pack(1)
-    index_rows()
+    index_cols()
     pass_upper(0)
     pass_lower(0)
+    hops(1)
     pass_upper(1)
-    hops(1)
+    x_far(0)
     pass_lower_again(0)
     send_lower(1)
+    hops(2)
     build_hot(0)
-    hops(2)
+    x_far(1)
+    hops(3)
     all_c(0).wait_recv()
     widen(0)
     schur_copy.wait()
-    hops(3)
     wait_upper(0)
     contribute(0)
-    exchange(0)
     for step in range(DIRECT, steps):
         hop_wait(step, 4)
     x_spread(2)
+    exchange(0)
     pass_lower(1)
     wait_upper(1)
     contribute(1)
     exchange(1)
+    x_far(2)
     x_spread(3)
     pass_lower_again(1)
     wait_upper(2)
     contribute(2)
     exchange(2)
-    x_spread(4)
     all_c(1).wait_recv()
     widen(1)
     build_hot(1)
+    x_far(3)
+    x_spread(4)
     collect(0, 0)
-    collect(0, 1)
     wait_upper(3)
     contribute(3)
     exchange(3)
+    x_far(4)
     collect(1, 0)
-    collect(1, 1)
     wait_upper(4)
     contribute(4)
     exchange(4)
     for step in range(2, steps):
-        for group in range(GROUPS):
+        for group in range(GROUPS[step]):
             collect(step, group)
 
     for step in range(steps):
@@ -514,7 +545,6 @@
     steps = len(STEPS)
     full = depth * count
     zs = count // X
-    members = count // GROUPS
     dims = (count, cols, rows, width, depth, cap)
     widths = [width // 4 * number for _, _, number in STEPS]
     half = width // 2
@@ -535,29 +565,28 @@
         cols_info=pltpu.VMEM((rows, 8), F32),
         place_info=pltpu.VMEM((children, count, TILE), F32),
         scale_col=pltpu.VMEM((rows, TILE), BF16),
-        high=pltpu.VMEM((rows, half), BF16),
-        low=pltpu.VMEM((rows, half), BF16),
+        both=pltpu.VMEM((rows, 2 * half), BF16),
         code_out=[pltpu.VMEM((slots, w), jnp.int16) for w in widths],
         code_in=[pltpu.VMEM((slots, w), jnp.int16) for w in widths],
         meta_out=pltpu.VMEM((steps, count, 1, TILE), F32),
         meta_in=pltpu.VMEM((steps, count, 1, TILE), F32),
-        meta_flat=pltpu.VMEM((members, TILE), F32),
-        spread=pltpu.VMEM((2, TILE, members * cap), BF16),
-        high_in=pltpu.VMEM((members * cap, half), BF16),
-        low_in=pltpu.VMEM((members * cap, half), BF16),
+        meta_flat=pltpu.VMEM((count, TILE), F32),
+        spread=pltpu.VMEM((2, TILE, slots), BF16),
+        both_in=pltpu.VMEM((slots, 2 * half), BF16),
         local_sem=dma((18,)),
         z_send=dma((steps,)),
         z_recv=dma((steps, zs)),
         x_send=dma((steps,)),
-        x_recv=dma((steps,)),
+        x_recv=dma((steps, 2, 2)),
+        far_recv=dma((steps,)),
         y_send=dma((children, 2, 2, 2)),
         y_recv=dma((children, 2, 2, 2)),
         c_send=dma((children,)),
         c_recv=dma((children,)),
         e_send=dma((steps,)),
-        e_recv=dma((steps, GROUPS)),
+        e_recv=dma((steps, max(GROUPS))),
         m_send=dma((steps,)),
-        m_recv=dma((steps, GROUPS)),
+        m_recv=dma((steps, max(GROUPS))),
     )
     added = pl.pallas_call(
         functools.partial(kernel, dims),
@@ -568,7 +597,13 @@
         compiler_params=pltpu.CompilerParams(
             collective_id=0, has_side_effects=True, vmem_limit_bytes=50 * 2**20
         ),
-    )(lower, upper, jnp.swapaxes(tile_mask, 1, 2), row_map, schur)
+    )(
+        pltpu.with_memory_space_constraint(lower, pltpu.HBM),
+        pltpu.with_memory_space_constraint(upper, pltpu.HBM),
+        jnp.swapaxes(tile_mask, 1, 2),
+        pltpu.with_memory_space_constraint(row_map, pltpu.HBM),
+        schur,
+    )
     return front + added
 
 

time: 124 us -> 110 us (0.89)
  Pallas kernels: 118 us -> 106 us
  local copies, waits for them, and re-layouts: 3.51 us -> 0.68 us
    pallas_call x1, Pallas kernels: 118 us -> 106 us  [shards(): pl.pallas_call(functools.partial(kernel, dims), out_shape=jax.ShapeDtypeS...]
    unnamed x10 -> x4, local copies, waits for them, and re-layouts: 3.51 us -> 0.68 us
where the time goes in v3:
time: 110 us; the launch traced here: 108 us
  Pallas kernels  106 us (96%)
  other arithmetic  1.8 us (2%)
    pallas_call x1, Pallas kernels, shards(): pl.pallas_call(functools.partial(kernel, dims), out_shape=jax.ShapeDtypeS...  106 us

profile of v3, /device:TPU:16, one launch (start us, length us, event | category | flops | bytes accessed | tf_op | source)
XLA Modules:
  0.0 108.3 jit_solution(17410832908614729079)
XLA Ops:
  0.0 0.0 copy-start
  0.0 0.7 copy-done
  0.7 0.0 copy-start.1
  0.7 105.8 %shard_map.64 = f32[1024,512]{1,0:T(8,128)S(1)} custom-call(bf16[2,1024,256]{2,1,0:T(8,128)(2,1)} %lower_hbm.1, bf16[2,64,512]{2,1,0:T(8,128)(2,1)} %upper_hbm.1, s32[2,2,8]{2,1,0:T(2,128)S(1)} %bitcast.1, s32[2,1024]{1,0:T(2,128)} %map_ref.1, f32[2,1024,512]{2,1,0:T(8,128)} %schur_hbm.1), custom_call_target="tpu_custom_call" | custom-call | tf_op jit(solution)/shard_map/pallas_call | solution.py:591
  106.4 0.0 copy-done.1
  106.5 1.8 %add.3 = f32[1024,512]{1,0:T(8,128)} add(f32[1024,512]{1,0:T(8,128)S(1)} %copy-done.1, f32[1024,512]{1,0:T(8,128)S(1)} %shard_map.64) | non-fusion elementwise | flops 524288 | bytes 6291456 | tf_op jit(solution)/shard_map/add | solution.py:607
Async XLA Ops:
  0.0 0.7 copy-start
  0.7 105.8 %copy-start.1 = (f32[1024,512]{1,0:T(8,128)S(1)}, f32[1024,512]{1,0:T(8,128)}, u32[]{:S(2)}) copy-start(f32[1024,512]{1,0:T(8,128)} %param.11) | copy-start | bytes 6291460

commit v4 on v3

--- a/solution.py
+++ b/solution.py
@@ -464,7 +464,6 @@
     lower_copy.wait()
     upper_copy.wait()
     pack(0)
-    index_rows()
     pl.semaphore_wait(barrier, count + cols - 2)
     send_upper(0)
     send_lower(0)
@@ -472,6 +471,7 @@
     for step in range(DIRECT, steps):
         hop_send(step, 1)
     pack(1)
+    index_rows()
     index_cols()
     pass_upper(0)
     pass_lower(0)
@@ -488,10 +488,10 @@
     widen(0)
     schur_copy.wait()
     wait_upper(0)
-    contribute(0)
     for step in range(DIRECT, steps):
         hop_wait(step, 4)
     x_spread(2)
+    contribute(0)
     exchange(0)
     pass_lower(1)
     wait_upper(1)
@@ -600,7 +600,7 @@
     )(
         pltpu.with_memory_space_constraint(lower, pltpu.HBM),
         pltpu.with_memory_space_constraint(upper, pltpu.HBM),
-        jnp.swapaxes(tile_mask, 1, 2),
+        pltpu.with_memory_space_constraint(jnp.swapaxes(tile_mask, 1, 2), pltpu.HBM),
         pltpu.with_memory_space_constraint(row_map, pltpu.HBM),
         schur,
     )

time: 110 us -> 108 us (0.982); the launches traced: 108 us -> 108 us
  no operation moved by 1% of the time
where the time goes in v4:
time: 108 us
  Pallas kernels  106 us (98%)
  other arithmetic  1.8 us (2%)
    pallas_call x1, Pallas kernels, shards(): pl.pallas_call(functools.partial(kernel, dims), out_shape=jax.ShapeDtypeS...  106 us

profile of v4, /device:TPU:16, one launch (start us, length us, event | category | flops | bytes accessed | tf_op | source)
XLA Modules:
  0.0 107.7 jit_solution(592689313082804888)
XLA Ops:
  0.0 0.0 copy-start
  0.0 105.9 %shard_map.64 = f32[1024,512]{1,0:T(8,128)S(1)} custom-call(bf16[2,1024,256]{2,1,0:T(8,128)(2,1)} %lower_hbm.1, bf16[2,64,512]{2,1,0:T(8,128)(2,1)} %upper_hbm.1, s32[2,2,8]{2,1,0:T(2,128)} %bitcast.1, s32[2,1024]{1,0:T(2,128)} %map_ref.1, f32[2,1024,512]{2,1,0:T(8,128)} %schur_hbm.1), custom_call_target="tpu_custom_call" | custom-call | tf_op jit(solution)/shard_map/pallas_call | solution.py:591
  105.9 0.0 copy-done
  105.9 1.8 %add.3 = f32[1024,512]{1,0:T(8,128)} add(f32[1024,512]{1,0:T(8,128)S(1)} %copy-done, f32[1024,512]{1,0:T(8,128)S(1)} %shard_map.64) | non-fusion elementwise | flops 524288 | bytes 6291456 | tf_op jit(solution)/shard_map/add | solution.py:607
Async XLA Ops:
  0.0 105.9 %copy-start = (f32[1024,512]{1,0:T(8,128)S(1)}, f32[1024,512]{1,0:T(8,128)}, u32[]{:S(2)}) copy-start(f32[1024,512]{1,0:T(8,128)} %param.11) | copy-start | bytes 6291460

commit v5 on v4

--- a/solution.py
+++ b/solution.py
@@ -12,7 +12,7 @@
 CORES = 2
 STEPS = ((0, 0, 1), (0, 1, 1), (0, 2, 2), (1, 0, 2), (1, 2, 2))
 DIRECT = 2
-GROUPS = (1, 1, 1, 1, 4)
+GROUPS = (1, 1, 1, 1, 8)
 MESH = pl.DeviceIdType.MESH
 F32 = jnp.float32
 BF16 = jnp.bfloat16

time: 108 us -> 108 us (level)
  no operation moved by 1% of the time
where the time goes in v5:
time: 108 us
  Pallas kernels  106 us (98%)
  other arithmetic  1.8 us (2%)
    pallas_call x1, Pallas kernels, shards(): pl.pallas_call(functools.partial(kernel, dims), out_shape=jax.ShapeDtypeS...  106 us

profile of v5, /device:TPU:16, one launch (start us, length us, event | category | flops | bytes accessed | tf_op | source)
XLA Modules:
  0.0 107.8 jit_solution(10329139093437043094)
XLA Ops:
  0.0 0.0 copy-start
  0.0 106.0 %shard_map.64 = f32[1024,512]{1,0:T(8,128)S(1)} custom-call(bf16[2,1024,256]{2,1,0:T(8,128)(2,1)} %lower_hbm.1, bf16[2,64,512]{2,1,0:T(8,128)(2,1)} %upper_hbm.1, s32[2,2,8]{2,1,0:T(2,128)} %bitcast.1, s32[2,1024]{1,0:T(2,128)} %map_ref.1, f32[2,1024,512]{2,1,0:T(8,128)} %schur_hbm.1), custom_call_target="tpu_custom_call" | custom-call | tf_op jit(solution)/shard_map/pallas_call | solution.py:591
  106.0 0.0 copy-done
  106.1 1.8 %add.3 = f32[1024,512]{1,0:T(8,128)} add(f32[1024,512]{1,0:T(8,128)S(1)} %copy-done, f32[1024,512]{1,0:T(8,128)S(1)} %shard_map.64) | non-fusion elementwise | flops 524288 | bytes 6291456 | tf_op jit(solution)/shard_map/add | solution.py:607
Async XLA Ops:
  0.0 106.0 %copy-start = (f32[1024,512]{1,0:T(8,128)S(1)}, f32[1024,512]{1,0:T(8,128)}, u32[]{:S(2)}) copy-start(f32[1024,512]{1,0:T(8,128)} %param.11) | copy-start | bytes 6291460
